TPU v7x, 32 devices: a whole 2x2x4 slice. The times are simulated.
32 devices in a mesh: seq: 4 (over z), chan: 8 (over y, x, core).
Axes of the slice: x: 2, y: 2, z: 4, core: 2. Of those that a mesh axis runs over, the one named last changes fastest.
Arguments:
- q_mr: bfloat16 [2048, 8192], P('seq', 'chan'), may hold values from -6 to 6
- k_mr: bfloat16 [2048, 8192], P('seq', 'chan'), may hold values from -6 to 6
- v_mr: bfloat16 [2048, 8192], P('seq', 'chan')
- q_lr: bfloat16 [2048, 8192], P('seq', 'chan'), may hold values from -6 to 6
- k_lr: bfloat16 [2048, 8192], P('seq', 'chan'), may hold values from -6 to 6
- cotangent: bfloat16 [2048, 8192], P('seq', 'chan'), may hold values from -6 to 6
- mr_filter: bfloat16 [128, 512], P(None, 'chan'), may hold values from -0.5 to 0.5
- decay_rates: float32 [16, 512], P(None, 'chan'), as said below
- residues: float32 [16, 512], P(None, 'chan'), may hold values from -1.5 to 1.5
- norm_gain: float32 [8192], P('chan'), may hold values from 0.1 to 1.9
Outputs:
- grad_q_mr: bfloat16 [2048, 8192], P('seq', 'chan')
- grad_k_mr: bfloat16 [2048, 8192], P('seq', 'chan')
- grad_v_mr: bfloat16 [2048, 8192], P('seq', 'chan')
- grad_q_lr: bfloat16 [2048, 8192], P('seq', 'chan')
- grad_k_lr: bfloat16 [2048, 8192], P('seq', 'chan')
- grad_filter: float32 [128, 512], P(None, 'chan')
- grad_residues: float32 [16, 512], P(None, 'chan')
- grad_gain: float32 [8192], P('chan')
Inputs may be any that keep to these rules, and one draw needn't show every extreme that they name: `decay_rates`: positive decay rates.
All inputs are finite; a program needn't handle non-finite values.
Results may differ from a plain program's by a relative error of at most 0.02.
Values may be sent and summed in bfloat16 or wider, within the bound.
No kernel may reach another device: no remote copies, remote signals or barrier semaphores. Data moves between devices by JAX's collectives and lax.ppermute only.
A program may use at most 192 MiB of HBM per device.

v0:
```python
import functools

import jax
import jax.numpy as jnp
from jax import lax
from jax.experimental import pallas as pl
from jax.experimental.pallas import tpu as pltpu
from jax.sharding import PartitionSpec as P

EPSILON = 1e-05
LANES = 128
F32 = jnp.float32
BF16 = jnp.bfloat16
VMEM_LIMIT = 48 * 1024 * 1024


def iota(shape, dim):
    return lax.broadcasted_iota(jnp.int32, shape, dim)


def dot(a, b):
    return jnp.dot(a, b, preferred_element_type=F32)


def dot_t(a, b, precision=None):
    return lax.dot_general(
        a, b, (((1,), (1,)), ((), ())), preferred_element_type=F32, precision=precision
    )


def scale_of(rates):
    twice = 2.0 * rates
    small = jnp.minimum(twice, 0.5)
    series = jnp.full_like(small, 1.0 / 40320.0)
    for term in (5040.0, 720.0, 120.0, 24.0, 6.0, 2.0, 1.0):
        series = 1.0 / term - small * series
    return jnp.sqrt(jnp.where(twice < 0.5, small * series, 1.0 - jnp.exp(-twice)))


def pick_column(rows, group_first, width):
    modes = rows.shape[0]
    tiled = jnp.concatenate([rows] * (LANES // width), axis=0)
    shape = tiled.shape
    chosen = iota(shape, 1) == group_first + iota(shape, 0) // modes
    return jnp.sum(jnp.where(chosen, tiled, 0.0), axis=1, keepdims=True)


def pick_groups(rows, mode, group_first, count):
    shape = (count, rows.shape[1])
    chosen = iota(shape, 1) == group_first + iota(shape, 0)
    row = jnp.broadcast_to(rows[mode : mode + 1, :], shape)
    return jnp.sum(jnp.where(chosen, row, 0.0), axis=1, keepdims=True)


def pick_channels(rows, group_first, width):
    modes = rows.shape[0]
    shape = (modes, LANES)
    total = jnp.zeros(shape, F32)
    for g in range(LANES // width):
        column = jnp.sum(
            jnp.where(iota(rows.shape, 1) == group_first + g, rows, 0.0), axis=1, keepdims=True
        )
        total = jnp.where(iota(shape, 1) // width == g, column, total)
    return total


def as_row(column):
    return jnp.transpose(jnp.broadcast_to(column, (LANES, LANES)))[0:1, :]


def fold_states(table, values, modes, width):
    full = dot(table, values)
    keep = iota(full.shape, 0) // modes == iota(full.shape, 1) // width
    full = jnp.where(keep, full, 0.0)
    total = full[0:modes]
    for g in range(1, LANES // width):
        total = total + full[g * modes : (g + 1) * modes]
    return total


def spread_states(states, width):
    modes = states.shape[0]
    tiled = jnp.concatenate([states] * (LANES // width), axis=0)
    keep = iota(tiled.shape, 0) // modes == iota(tiled.shape, 1) // width
    return jnp.where(keep, tiled, 0.0).astype(BF16)


def carry(received, rates_c, rows):
    total = received[0]
    for k in range(1, len(received)):
        total = total + jnp.exp(rates_c * (-float(rows * k))) * received[k]
    return total


def skew(row, taps):
    wide = jnp.broadcast_to(row, (taps, row.shape[1]))
    return pltpu.roll(wide, 0, 1, stride=1, stride_axis=0)


def unskew_sum(grid):
    rows, size = grid.shape
    while rows > 8:
        half = rows // 2
        grid = grid[:half] + pltpu.roll(grid[half:], size - half, 1)
        rows = half
    for bit in (1, 2, 4):
        moved = (iota(grid.shape, 0) // bit) % 2 == 1
        grid = jnp.where(moved, pltpu.roll(grid, size - bit, 1), grid)
    return jnp.sum(grid, axis=0, keepdims=True)


def keep_group(values, g, width):
    return jnp.where((iota(values.shape, 1) % LANES) // width == g, values, jnp.zeros_like(values))


def prep_kernel(width, cot, q_lr, rates_ref, res_ref, filt, states, h_out, hr_out, taps_out):
    i = pl.program_id(0)
    rows = cot.shape[0]
    taps = filt.shape[0]
    rates = rates_ref[...]
    modes = rates.shape[0]
    count = LANES // width
    first = i * count
    scaled = res_ref[...] * scale_of(rates)
    column = pick_column(rates, first, width)
    powers = jnp.exp(-column * iota((LANES, rows), 1).astype(F32)).astype(BF16)
    grad = (cot[...].astype(F32) * q_lr[...].astype(F32)).astype(BF16)
    states[...] = fold_states(powers, grad, modes, width)
    forward = iota((count, rows), 1)
    backward = rows - taps - forward
    backward = jnp.where(backward < 0, backward + rows, backward)
    forward = forward.astype(F32)
    backward = backward.astype(F32)
    h = jnp.zeros((count, rows), F32)
    hr = jnp.zeros((count, rows), F32)
    for n in range(modes):
        rate = pick_groups(rates, n, first, count)
        amount = pick_groups(scaled, n, first, count)
        h = h + amount * jnp.exp(-rate * forward)
        hr = hr + amount * jnp.exp(-rate * backward)
    h_out[...] = h
    hr_out[...] = hr

    @pl.when(i == 0)
    def _():
        lane = iota((taps, 4 * taps), 1)
        tap = iota((taps, 4 * taps), 0)
        chosen = jnp.logical_or(lane == tap, lane == 3 * taps - tap)
        select = jnp.where(chosen, 1.0, 0.0).astype(BF16)
        taps_out[...] = lax.dot_general(
            filt[...], select, (((0,), (0,)), ((), ())), preferred_element_type=F32
        )


def back_kernel(width, taps, cot, q_lr, h, out, near, far, data):
    grad = (cot[...].astype(F32) * q_lr[...].astype(F32)).astype(BF16)
    half = 2 * taps
    zero = jnp.zeros((taps, taps), BF16)
    later = iota((taps, taps), 1) >= iota((taps, taps), 0)
    for g in range(LANES // width):
        table = skew(h[g : g + 1, :], taps)
        part = [table[:, taps * d : taps * (d + 1)] for d in range(4)]
        part[0] = jnp.where(later, part[0], 0.0)
        part = [p.astype(BF16) for p in part]
        lo = g * half
        near[0:taps, lo : lo + taps] = part[0]
        near[0:taps, lo + taps : lo + half] = part[1]
        near[taps:half, lo : lo + taps] = zero
        near[taps:half, lo + taps : lo + half] = part[0]
        far[0:taps, lo : lo + taps] = part[2]
        far[0:taps, lo + taps : lo + half] = part[3]
        far[taps:half, lo : lo + taps] = part[1]
        far[taps:half, lo + taps : lo + half] = part[2]
        kept = keep_group(grad, g, width)
        data[lo : lo + half, 0:LANES] = kept[0:half]
        data[lo : lo + half, LANES : 2 * LANES] = kept[half:]
    own = dot(near[...], data[...])
    other = dot(far[...], data[:, LANES:])
    out[0:half, :] = own[:, 0:LANES] + other
    out[half:, :] = own[:, LANES:]


def medium_kernel(width, peers, *refs):
    (q, k, v, edge, taps_rows, local, k_lr, gain, rates_ref, res_ref) = refs[:10]
    received = refs[10 : 10 + peers]
    conv, grad_w, sums, table, data, acc_y, acc_n = refs[10 + peers :]
    i = pl.program_id(0)
    rows = q.shape[0]
    taps = edge.shape[0]
    blocks = rows // taps
    count = LANES // width
    first = i * count
    rates = rates_ref[...]
    scaled = res_ref[...] * scale_of(rates)
    kv = (k[...].astype(F32) * v[...].astype(F32)).astype(BF16)
    joined = jnp.concatenate([edge[...], kv], axis=0)
    for g in range(count):
        lo = g * 2 * taps
        table[:, lo : lo + 2 * taps] = skew(taps_rows[g : g + 1, :], taps).astype(BF16)
        kept = keep_group(joined, g, width)
        for b in range(blocks):
            data[lo : lo + 2 * taps, b * LANES : (b + 1) * LANES] = kept[b * taps : (b + 2) * taps]
    result = dot(table[...], data[...])
    column = pick_column(rates, first, width)
    states = carry([r[...] for r in received], pick_channels(rates, first, width), rows)
    states = states * pick_channels(scaled, first, width)
    reach = (rows - iota((rows, LANES), 0)).astype(F32)
    powers = jnp.exp(-as_row(column) * reach).astype(BF16)
    total = local[...] + dot(powers, spread_states(states, width))
    grad_w[...] = total

    @pl.when(i == 0)
    def _():
        acc_y[...] = jnp.zeros_like(acc_y)
        acc_n[...] = jnp.zeros_like(acc_n)

    for b in range(blocks):
        part = slice(b * taps, (b + 1) * taps)
        z = result[:, b * LANES : (b + 1) * LANES]
        conv[part, :] = z
        y = q[part, :].astype(F32) * z
        grad_normed = total[part, :] * k_lr[part, :].astype(F32) * gain[...]
        acc_y[part, :] += y * y
        acc_n[part, :] += grad_normed * y

    @pl.when(i == pl.num_programs(0) - 1)
    def _():
        ones = jnp.ones((8, LANES), F32)
        low = iota((8, rows), 0) < 4
        sums[...] = jnp.where(
            low,
            dot_t(ones, acc_y[...], lax.Precision.HIGHEST),
            dot_t(ones, acc_n[...], lax.Precision.HIGHEST),
        )


def norm_kernel(width, model_width, sharers, *refs):
    q, k_lr, conv, grad_w, gain, rates_ref = refs[:6]
    parts = refs[6 : 6 + sharers]
    w, grad_z, grad_edge, grad_k, grad_q, gain_part, states, inv_ref, inner_ref = refs[6 + sharers :]
    i = pl.program_id(0)
    rows = q.shape[0]
    taps = grad_edge.shape[0]
    rates = rates_ref[...]
    modes = rates.shape[0]

    @pl.when(i == 0)
    def _():
        total = parts[0][...]
        for part in parts[1:]:
            total = total + part[...]
        total = total / model_width
        inv = 1.0 / jnp.sqrt(total[0:1, :] + EPSILON)
        inner = total[7:8, :] * inv
        inv_ref[...] = jnp.transpose(jnp.broadcast_to(inv, (LANES, rows)))
        inner_ref[...] = jnp.transpose(jnp.broadcast_to(inner, (LANES, rows)))

    q_f = q[...].astype(F32)
    k_f = k_lr[...].astype(F32)
    z = conv[...]
    gw = grad_w[...]
    inv = inv_ref[...]
    normed = q_f * z * inv
    v_lr = (normed * gain[...]).astype(BF16).astype(F32)
    w_lr = (k_f * v_lr).astype(BF16)
    w[...] = w_lr
    grad_k[...] = (gw * v_lr).astype(BF16)
    grad_v = gw * k_f
    gain_part[...] = jnp.sum(grad_v * normed, axis=0, keepdims=True)
    grad_y = (grad_v * gain[...] - normed * inner_ref[...]) * inv
    grad_q[...] = (grad_y * z).astype(BF16)
    grad_conv = (grad_y * q_f).astype(BF16)
    grad_z[...] = grad_conv
    grad_edge[...] = grad_conv[0:taps]
    column = pick_column(rates, i * (LANES // width), width)
    reach = (rows - 1 - iota((LANES, rows), 1)).astype(F32)
    states[...] = fold_states(jnp.exp(-column * reach).astype(BF16), w_lr, modes, width)


def cross_kernel(
    width, grad_z, k, v, edge, cot, q_lr, w, rates_ref, gain_part, pack, left, right, wide, lags
):
    i = pl.program_id(0)
    rows = k.shape[0]
    taps = edge.shape[0]
    blocks = rows // taps
    count = LANES // width
    rates = rates_ref[...]
    modes = rates.shape[0]
    groups = rates.shape[1]
    kv = (k[...].astype(F32) * v[...].astype(F32)).astype(BF16)
    joined = jnp.concatenate([edge[...], kv], axis=0)
    gz = grad_z[...]
    side = jnp.concatenate([gz[b * taps : (b + 1) * taps] for b in range(blocks)], axis=1)
    for g in range(count):
        left[g * taps : (g + 1) * taps, :] = keep_group(side, g, width)
    for b in range(blocks):
        right[:, b * LANES : (b + 1) * LANES] = joined[b * taps : (b + 2) * taps]
    grid = dot_t(left[...], right[...])
    rows_out = [unskew_sum(grid[g * taps : (g + 1) * taps]) for g in range(count)]
    found = pltpu.roll(jnp.concatenate(rows_out, axis=0), 2 * taps - 1, 1)
    pack[pl.ds(pl.multiple_of(i * count, count), count), :] = found[:, 0:taps]
    grad = (cot[...].astype(F32) * q_lr[...].astype(F32)).astype(BF16)
    side = jnp.concatenate([grad[b * taps : (b + 1) * taps] for b in range(blocks)], axis=1)
    for g in range(count):
        left[g * taps : (g + 1) * taps, :] = keep_group(side, g, width)
    zero = jnp.zeros((taps, LANES), BF16)
    for d in range(blocks):
        at = (blocks - 1 - d) * taps
        for b in range(blocks):
            value = zero if b < d else w[(b - d) * taps : (b - d + 1) * taps, :]
            wide[at : at + taps, b * LANES : (b + 1) * LANES] = value
    lags[...] = dot_t(left[...], wide[...])
    last = rows - taps
    shape = (taps, rows)
    causal = iota(shape, 1) - last <= iota(shape, 0)
    found = [
        unskew_sum(jnp.where(causal, lags[g * taps : (g + 1) * taps, :], 0.0)) for g in range(count)
    ]
    found = jnp.concatenate(found, axis=0)
    lag = last - iota(found.shape, 1)
    lag = jnp.where(lag < 0, lag + rows, lag).astype(F32)
    result = jnp.zeros((count, LANES), F32)
    for n in range(modes):
        rate = pick_groups(rates, n, i * count, count)
        value = jnp.sum(jnp.exp(-rate * lag) * found, axis=1, keepdims=True)
        result = jnp.where(iota(result.shape, 1) == n, value, result)
    pack[pl.ds(pl.multiple_of(groups + i * count, count), count), :] = result
    pack[pl.ds(2 * groups + i, 1), :] = gain_part[...]


def join_kernel(width, rows, peers, *refs):
    pack, states, rates_ref = refs[:3]
    received = refs[3 : 3 + peers]
    out = refs[3 + peers]
    rates = rates_ref[...]
    modes, groups = rates.shape
    count = LANES // width
    out[...] = pack[...]
    for i in range(groups // count):
        part = slice(i * LANES, (i + 1) * LANES)
        rates_c = pick_channels(rates, i * count, width)
        carried = carry([r[:, part] for r in received], rates_c, rows)
        product = jnp.exp(-rates_c) * carried * states[:, part]
        shape = (LANES, LANES)
        member = jnp.where(iota((count, LANES), 1) // width == iota((count, LANES), 0), 1.0, 0.0)
        padded = jnp.concatenate([product, jnp.zeros((LANES - modes, LANES), F32)], axis=0)
        at = groups + i * count
        out[at : at + count, :] += dot_t(member, padded, lax.Precision.HIGHEST)


def last_kernel(width, peers, *refs):
    (w, cot, hr, taps_rows, grad_z, after, k, v, rates_ref, res_ref) = refs[:10]
    received = refs[10 : 10 + peers]
    grad_q, grad_k, grad_v, near, far, data, table, wide = refs[10 + peers :]
    i = pl.program_id(0)
    rows = w.shape[0]
    taps = after.shape[0]
    blocks = rows // taps
    half = 2 * taps
    count = LANES // width
    first = i * count
    rates = rates_ref[...]
    scaled = res_ref[...] * scale_of(rates)
    zero = jnp.zeros((taps, taps), BF16)
    earlier = iota((taps, taps), 1) <= iota((taps, taps), 0)
    w_lr = w[...]
    joined = jnp.concatenate([grad_z[...], after[...]], axis=0)
    for g in range(count):
        rolled = skew(hr[g : g + 1, :], taps)
        part = [rolled[:, taps * (3 - d) : taps * (4 - d)] for d in range(4)]
        part[0] = jnp.where(earlier, part[0], 0.0)
        part = [p.astype(BF16) for p in part]
        lo = g * half
        near[0:taps, lo : lo + taps] = part[0]
        near[0:taps, lo + taps : lo + half] = zero
        near[taps:half, lo : lo + taps] = part[1]
        near[taps:half, lo + taps : lo + half] = part[0]
        far[0:taps, lo : lo + taps] = part[2]
        far[0:taps, lo + taps : lo + half] = part[1]
        far[taps:half, lo : lo + taps] = part[3]
        far[taps:half, lo + taps : lo + half] = part[2]
        kept = keep_group(w_lr, g, width)
        data[lo : lo + half, 0:LANES] = kept[0:half]
        data[lo : lo + half, LANES : 2 * LANES] = kept[half:]
        table[:, lo : lo + half] = skew(taps_rows[g : g + 1, :], taps).astype(BF16)
        kept = keep_group(joined, g, width)
        for b in range(blocks):
            wide[lo : lo + half, b * LANES : (b + 1) * LANES] = kept[b * taps : (b + 2) * taps]
    own = dot(near[...], data[...])
    other = dot(far[...], data[:, 0:LANES])
    column = pick_column(rates, first, width)
    states = carry([r[...] for r in received], pick_channels(rates, first, width), rows)
    states = states * pick_channels(scaled, first, width)
    reach = (1 + iota((rows, LANES), 0)).astype(F32)
    powers = jnp.exp(-as_row(column) * reach).astype(BF16)
    outer = dot(powers, spread_states(states, width))
    grad_out = cot[...].astype(F32)
    grad_q[0:half, :] = (grad_out[0:half] * (own[:, 0:LANES] + outer[0:half])).astype(BF16)
    grad_q[half:, :] = (grad_out[half:] * (own[:, LANES:] + other + outer[half:])).astype(BF16)
    result = dot(table[...], wide[...])
    for b in range(blocks):
        part = slice(b * taps, (b + 1) * taps)
        grad_kv = result[:, b * LANES : (b + 1) * LANES]
        grad_k[part, :] = (grad_kv * v[part, :].astype(F32)).astype(BF16)
        grad_v[part, :] = (grad_kv * k[part, :].astype(F32)).astype(BF16)


def close_kernel(sharers, norm_terms, gain_terms, *refs):
    rates_ref = refs[0]
    packs = [r[...] for r in refs[1 : 1 + sharers]]
    taps_out, modes_out, gain_out = refs[1 + sharers :]
    while len(packs) > 1:
        half = len(packs) // 2
        if len(packs) % 2:
            packs = [packs[0] + packs[-1]] + packs[1:-1]
        else:
            packs = [packs[j] + packs[j + half] for j in range(half)]
    total = packs[0]
    rates = rates_ref[...]
    modes, groups = rates.shape
    taps = taps_out.shape[0]
    square = (taps, LANES)
    reverse = jnp.where(iota(square, 0) + iota(square, 1) == taps - 1, 1.0, 0.0)
    found = dot_t(reverse, total[0:groups], lax.Precision.HIGHEST)
    taps_out[...] = found * (1.0 / norm_terms)
    shape = (modes, LANES)
    same = jnp.where(iota(shape, 0) == iota(shape, 1), 1.0, 0.0)
    found = dot_t(same, total[groups : 2 * groups], lax.Precision.HIGHEST)
    modes_out[...] = found * scale_of(rates) * (1.0 / norm_terms)
    gain_out[...] = total[2 * groups :] * (1.0 / gain_terms)


def shifted(value, axis, steps):
    count = lax.axis_size(axis)
    first, last = max(0, -steps), min(count, count - steps)
    return lax.ppermute(value, axis, [(source, source + steps) for source in range(first, last)])


def rotated(value, axis, steps):
    count = lax.axis_size(axis)
    return lax.ppermute(value, axis, [(source, (source - steps) % count) for source in range(count)])


def shards(q_mr, k_mr, v_mr, q_lr, k_lr, cotangent, mr_filter, decay_rates, residues, norm_gain):
    rows, chans = q_mr.shape
    taps, groups = mr_filter.shape
    modes = decay_rates.shape[0]
    width = chans // groups
    count = LANES // width
    steps = chans // LANES
    seq_count = lax.axis_size("seq")
    chan_count = lax.axis_size("chan")
    peers = seq_count - 1
    half = 2 * taps
    gain = norm_gain.reshape(1, chans)

    wide = pl.BlockSpec((rows, LANES), lambda i: (0, i))
    edge_spec = pl.BlockSpec((taps, LANES), lambda i: (0, i))
    state_spec = pl.BlockSpec((modes, LANES), lambda i: (0, i))
    line = pl.BlockSpec((1, LANES), lambda i: (0, i))
    h_spec = pl.BlockSpec((count, rows), lambda i: (i, 0))
    down = pl.BlockSpec((count, half), lambda i: (i, 0))
    up = pl.BlockSpec((count, half), lambda i: (i, 1))

    def whole(array):
        return pl.BlockSpec(array.shape, lambda i: (0,) * len(array.shape))

    def shape(dims, dtype):
        return jax.ShapeDtypeStruct(dims, dtype)

    params = pltpu.CompilerParams(
        dimension_semantics=("arbitrary",), vmem_limit_bytes=VMEM_LIMIT
    )

    key_edge = (k_mr[rows - taps :].astype(F32) * v_mr[rows - taps :].astype(F32)).astype(BF16)
    edge = shifted(key_edge, "seq", 1)

    small = shape((modes, chans), F32)
    back_states, h, hr, taps_rows = pl.pallas_call(
        functools.partial(prep_kernel, width),
        grid=(steps,),
        in_specs=[wide, wide, whole(decay_rates), whole(residues), whole(mr_filter)],
        out_specs=[state_spec, h_spec, h_spec, pl.BlockSpec((groups, 2 * half), lambda i: (0, 0))],
        out_shape=[
            small,
            shape((groups, rows), F32),
            shape((groups, rows), F32),
            shape((groups, 2 * half), F32),
        ],
        compiler_params=params,
        name="prep",
    )(cotangent, q_lr, decay_rates, residues, mr_filter)
    from_later = [shifted(back_states, "seq", -k) for k in range(1, seq_count)]

    local = pl.pallas_call(
        functools.partial(back_kernel, width, taps),
        grid=(steps,),
        in_specs=[wide, wide, h_spec],
        out_specs=wide,
        out_shape=shape((rows, chans), F32),
        scratch_shapes=[
            pltpu.VMEM((half, count * half), BF16),
            pltpu.VMEM((half, count * half), BF16),
            pltpu.VMEM((count * half, 2 * LANES), BF16),
        ],
        compiler_params=params,
        name="back",
    )(cotangent, q_lr, h)

    conv, grad_w, sums = pl.pallas_call(
        functools.partial(medium_kernel, width, peers),
        grid=(steps,),
        in_specs=[wide, wide, wide, edge_spec, up, wide, wide, line]
        + [whole(decay_rates), whole(residues)]
        + [state_spec] * peers,
        out_specs=[wide, wide, pl.BlockSpec((8, rows), lambda i: (0, 0))],
        out_shape=[shape((rows, chans), F32), shape((rows, chans), F32), shape((8, rows), F32)],
        scratch_shapes=[
            pltpu.VMEM((taps, count * half), BF16),
            pltpu.VMEM((count * half, (rows // taps) * LANES), BF16),
            pltpu.VMEM((rows, LANES), F32),
            pltpu.VMEM((rows, LANES), F32),
        ],
        compiler_params=params,
        name="medium",
    )(q_mr, k_mr, v_mr, edge, taps_rows, local, k_lr, gain, decay_rates, residues, *from_later)

    parts = [sums] + [rotated(sums, "chan", k) for k in range(1, chan_count)]
    w, grad_z, grad_edge, grad_k_lr, grad_q_mr, gain_part, states = pl.pallas_call(
        functools.partial(norm_kernel, width, float(chans * chan_count), chan_count),
        grid=(steps,),
        in_specs=[wide, wide, wide, wide, line, whole(decay_rates)] + [whole(sums)] * chan_count,
        out_specs=[wide, wide, edge_spec, wide, wide, line, state_spec],
        out_shape=[
            shape((rows, chans), BF16),
            shape((rows, chans), BF16),
            shape((taps, chans), BF16),
            shape((rows, chans), BF16),
            shape((rows, chans), BF16),
            shape((1, chans), F32),
            small,
        ],
        scratch_shapes=[pltpu.VMEM((rows, LANES), F32), pltpu.VMEM((rows, LANES), F32)],
        compiler_params=params,
        name="norm",
    )(q_mr, k_lr, conv, grad_w, gain, decay_rates, *parts)
    from_earlier = [shifted(states, "seq", k) for k in range(1, seq_count)]
    after = shifted(grad_edge, "seq", -1)

    pack_shape = (2 * groups + steps, LANES)
    pack = pl.pallas_call(
        functools.partial(cross_kernel, width),
        grid=(steps,),
        in_specs=[wide, wide, wide, edge_spec, wide, wide, wide, whole(decay_rates), line],
        out_specs=pl.BlockSpec(pack_shape, lambda i: (0, 0)),
        out_shape=shape(pack_shape, F32),
        scratch_shapes=[
            pltpu.VMEM((count * taps, (rows // taps) * LANES), BF16),
            pltpu.VMEM((half, (rows // taps) * LANES), BF16),
            pltpu.VMEM((rows, (rows // taps) * LANES), BF16),
            pltpu.VMEM((count * taps, rows), F32),
        ],
        compiler_params=params,
        name="cross",
    )(grad_z, k_mr, v_mr, edge, cotangent, q_lr, w, decay_rates, gain_part)

    pack = pl.pallas_call(
        functools.partial(join_kernel, width, rows, peers),
        out_shape=shape(pack_shape, F32),
        compiler_params=pltpu.CompilerParams(vmem_limit_bytes=VMEM_LIMIT),
        name="join",
    )(pack, back_states, decay_rates, *from_earlier)
    packs = [pack] + [rotated(pack, "seq", k) for k in range(1, seq_count)]

    grad_q_lr, grad_k_mr, grad_v_mr = pl.pallas_call(
        functools.partial(last_kernel, width, peers),
        grid=(steps,),
        in_specs=[wide, wide, h_spec, down, wide, edge_spec, wide, wide]
        + [whole(decay_rates), whole(residues)]
        + [state_spec] * peers,
        out_specs=[wide, wide, wide],
        out_shape=[shape((rows, chans), BF16)] * 3,
        scratch_shapes=[
            pltpu.VMEM((half, count * half), BF16),
            pltpu.VMEM((half, count * half), BF16),
            pltpu.VMEM((count * half, 2 * LANES), BF16),
            pltpu.VMEM((taps, count * half), BF16),
            pltpu.VMEM((count * half, (rows // taps) * LANES), BF16),
        ],
        compiler_params=params,
        name="last",
    )(w, cotangent, hr, taps_rows, grad_z, after, k_mr, v_mr, decay_rates, residues, *from_earlier)

    total_rows = rows * seq_count
    taps_sum, mode_sum, gain_sum = pl.pallas_call(
        functools.partial(
            close_kernel, seq_count, float(total_rows * width) ** 0.5, float(total_rows) ** 0.5
        ),
        out_shape=[shape((taps, groups), F32), shape((modes, groups), F32), shape((steps, LANES), F32)],
        compiler_params=pltpu.CompilerParams(vmem_limit_bytes=VMEM_LIMIT),
        name="close",
    )(decay_rates, *packs)
    return (
        grad_q_mr,
        grad_k_mr,
        grad_v_mr,
        grad_q_lr,
        grad_k_lr,
        taps_sum,
        mode_sum,
        gain_sum.reshape(chans),
    )


def solution(mesh):
    tile = P("seq", "chan")
    column = P(None, "chan")
    return jax.shard_map(
        shards,
        mesh=mesh,
        in_specs=(tile,) * 6 + (column,) * 3 + (P("chan"),),
        out_specs=(tile,) * 5 + (column,) * 2 + (P("chan"),),
        check_vma=False,
    )
```

profile of v0, /device:TPU:0, one launch (start us, length us, event | category | flops | bytes accessed | tf_op | source)
XLA Modules:
  0.0 122.2 jit_solution(10281249959614931388)
XLA Ops:
  1.7 4.9 %collective-permute-start = (bf16[128,1024]{1,0:T(8,128)(2,1)S(1)}, bf16[128,1024]{1,0:T(8,128)(2,1)S(1)}, u32[]{:S(2)}, u32[]{:S(2)}) collective-permute-start(bf16[128,1024]{1,0:T(8,128)(2,1)S(1)} %multiply_convert_fusion), channel_id=1, source_target_pairs={{0,8},{8,16},{16,24},{1,9},{9,17},{17,25},{2,10},{10,18},{18,26},{... | collective-permute-start | bytes 786440 | tf_op jit(solution)/shard_map/ppermute | solution.py:437
  11.4 2.9 %prep.1 = (f32[16,1024]{1,0:T(8,128)S(1)}, f32[64,512]{1,0:T(8,128)S(1)}, f32[64,512]{1,0:T(8,128)S(1)}, f32[64,512]{1,0:T(8,128)S(1)}) custom-call(bf16[512,1024]{1,0:T(8,128)(2,1)S(1)} %copy-done, bf16[512,1024]{1,0:T(8,128)(2,1)S(1)} %copy-done.4, f32[16,64]{1,0:T(8,128)S(1)} %copy-done.13, f32[16,64]{1,0:T(8,128)S(1)} %copy-done.23, ...), custom_call_target="tpu_custom_call" | custom-call | tf_op jit(solution)/shard_map/prep/pallas_call | solution.py:480
  14.3 1.3 %collective-permute-start.3 = (f32[16,1024]{1,0:T(8,128)S(1)}, f32[16,1024]{1,0:T(8,128)S(1)}, u32[]{:S(2)}, u32[]{:S(2)}) collective-permute-start(f32[16,1024]{1,0:T(8,128)S(1)} %get-tuple-element.30.refs_1_), channel_id=1, source_target_pairs={{24,0},{25,1},{26,2},{27,3},{28,4},{29,5},{30,6},{31,7}} | collective-permute-start | bytes 196616 | tf_op jit(solution)/shard_map/ppermute | solution.py:437
  15.6 1.3 %collective-permute-start.2 = (f32[16,1024]{1,0:T(8,128)S(1)}, f32[16,1024]{1,0:T(8,128)S(1)}, u32[]{:S(2)}, u32[]{:S(2)}) collective-permute-start(f32[16,1024]{1,0:T(8,128)S(1)} %get-tuple-element.30.refs_1_), channel_id=1, source_target_pairs={{16,0},{24,8},{17,1},{25,9},{18,2},{26,10},{19,3},{27,11},{20,4},{... | collective-permute-start | bytes 196616 | tf_op jit(solution)/shard_map/ppermute | solution.py:437
  16.9 1.3 %collective-permute-start.1 = (f32[16,1024]{1,0:T(8,128)S(1)}, f32[16,1024]{1,0:T(8,128)S(1)}, u32[]{:S(2)}, u32[]{:S(2)}) collective-permute-start(f32[16,1024]{1,0:T(8,128)S(1)} %get-tuple-element.30.refs_1_), channel_id=1, source_target_pairs={{8,0},{16,8},{24,16},{9,1},{17,9},{25,17},{10,2},{18,10},{26,18},{... | collective-permute-start | bytes 196616 | tf_op jit(solution)/shard_map/ppermute | solution.py:437
  18.3 8.2 %back.1.refs_5_ = f32[512,1024]{1,0:T(8,128)S(1)} custom-call(bf16[512,1024]{1,0:T(8,128)(2,1)S(1)} %copy-done, bf16[512,1024]{1,0:T(8,128)(2,1)S(1)} %copy-done.4, f32[64,512]{1,0:T(8,128)S(1)} %get-tuple-element.29.h), custom_call_target="tpu_custom_call" | custom-call | tf_op jit(solution)/shard_map/back/pallas_call | solution.py:496
  26.5 1.3 %copy-done.6 = f32[512,1024]{1,0:T(8,128)} copy-done((f32[512,1024]{1,0:T(8,128)}, f32[512,1024]{1,0:T(8,128)S(1)}, u32[]{:S(2)}) %copy-start.6) | copy-done | bytes 2097176
  27.9 11.1 %medium.1 = (f32[512,1024]{1,0:T(8,128)}, f32[512,1024]{1,0:T(8,128)}, f32[8,512]{1,0:T(8,128)S(1)}) custom-call(bf16[512,1024]{1,0:T(8,128)(2,1)S(1)} %copy-done.11, bf16[512,1024]{1,0:T(8,128)(2,1)S(1)} %copy-done.2, bf16[512,1024]{1,0:T(8,128)(2,1)S(1)} %copy-done.3, bf16[128,1024]{1,0:T(8,128)(2,1)S(1)} %collective-permute-done.refs_3_.edge, ...), custom_call_target="tpu_custom_call" | custom-call | tf_op jit(solution)/shard_map/medium/pallas_call | solution.py:511
  39.0 1.5 %collective-permute-start.9 = (f32[8,512]{1,0:T(8,128)S(1)}, f32[8,512]{1,0:T(8,128)S(1)}, u32[]{:S(2)}, u32[]{:S(2)}) collective-permute-start(f32[8,512]{1,0:T(8,128)S(1)} %get-tuple-element.33.refs_6_), channel_id=1, source_target_pairs={{0,2},{1,3},{2,4},{3,5},{4,6},{5,7},{6,0},{7,1},{8,10},{9,11},{10,... | collective-permute-start | bytes 49160 | tf_op jit(solution)/shard_map/ppermute | solution.py:442
  40.5 2.4 %collective-permute-start.8 = (f32[8,512]{1,0:T(8,128)S(1)}, f32[8,512]{1,0:T(8,128)S(1)}, u32[]{:S(2)}, u32[]{:S(2)}) collective-permute-start(f32[8,512]{1,0:T(8,128)S(1)} %get-tuple-element.33.refs_6_), channel_id=1, source_target_pairs={{0,3},{1,4},{2,5},{3,6},{4,7},{5,0},{6,1},{7,2},{8,11},{9,12},{10,... | collective-permute-start | bytes 49160 | tf_op jit(solution)/shard_map/ppermute | solution.py:442
  43.5 1.4 %collective-permute-start.5 = (f32[8,512]{1,0:T(8,128)S(1)}, f32[8,512]{1,0:T(8,128)S(1)}, u32[]{:S(2)}, u32[]{:S(2)}) collective-permute-start(f32[8,512]{1,0:T(8,128)S(1)} %get-tuple-element.33.refs_6_), channel_id=1, source_target_pairs={{0,6},{1,7},{2,0},{3,1},{4,2},{5,3},{6,4},{7,5},{8,14},{9,15},{10,... | collective-permute-start | bytes 49160 | tf_op jit(solution)/shard_map/ppermute | solution.py:442
  44.9 2.3 %collective-permute-start.4 = (f32[8,512]{1,0:T(8,128)S(1)}, f32[8,512]{1,0:T(8,128)S(1)}, u32[]{:S(2)}, u32[]{:S(2)}) collective-permute-start(f32[8,512]{1,0:T(8,128)S(1)} %get-tuple-element.33.refs_6_), channel_id=1, source_target_pairs={{0,7},{1,0},{2,1},{3,2},{4,3},{5,4},{6,5},{7,6},{8,15},{9,8},{10,9... | collective-permute-start | bytes 49160 | tf_op jit(solution)/shard_map/ppermute | solution.py:442
  47.3 1.4 %collective-permute-done.4.refs_7_ = f32[8,512]{1,0:T(8,128)S(1)} collective-permute-done((f32[8,512]{1,0:T(8,128)S(1)}, f32[8,512]{1,0:T(8,128)S(1)}, u32[]{:S(2)}, u32[]{:S(2)}) %collective-permute-start.4) | collective-permute-done | bytes 16416 | tf_op jit(solution)/shard_map/ppermute | solution.py:442
  48.7 8.1 %norm.1 = (bf16[512,1024]{1,0:T(8,128)(2,1)S(1)}, bf16[512,1024]{1,0:T(8,128)(2,1)S(1)}, bf16[128,1024]{1,0:T(8,128)(2,1)}, bf16[512,1024]{1,0:T(8,128)(2,1)}, b...) custom-call(bf16[512,1024]{1,0:T(8,128)(2,1)S(1)} %copy-done.11, ...), custom_call_target="tpu_custom_call" | custom-call | tf_op jit(solution)/shard_map/norm/pallas_call | solution.py:530
  57.8 1.3 %collective-permute-start.11 = (bf16[128,1024]{1,0:T(8,128)(2,1)}, bf16[128,1024]{1,0:T(8,128)(2,1)}, u32[]{:S(2)}, u32[]{:S(2)}) collective-permute-start(bf16[128,1024]{1,0:T(8,128)(2,1)} %get-tuple-element.38), channel_id=1, source_target_pairs={{8,0},{16,8},{24,16},{9,1},{17,9},{25,17},{10,2},{18,10},{26,18},{... | collective-permute-start | bytes 786440 | tf_op jit(solution)/shard_map/ppermute | solution.py:437
  59.1 8.8 %collective-permute-start.14 = (f32[16,1024]{1,0:T(8,128)S(1)}, f32[16,1024]{1,0:T(8,128)S(1)}, u32[]{:S(2)}, u32[]{:S(2)}) collective-permute-start(f32[16,1024]{1,0:T(8,128)S(1)} %get-tuple-element.39), channel_id=1, source_target_pairs={{0,24},{1,25},{2,26},{3,27},{4,28},{5,29},{6,30},{7,31}} | collective-permute-start | bytes 196616 | tf_op jit(solution)/shard_map/ppermute | solution.py:437
  67.9 1.3 %collective-permute-start.13 = (f32[16,1024]{1,0:T(8,128)S(1)}, f32[16,1024]{1,0:T(8,128)S(1)}, u32[]{:S(2)}, u32[]{:S(2)}) collective-permute-start(f32[16,1024]{1,0:T(8,128)S(1)} %get-tuple-element.39), channel_id=1, source_target_pairs={{0,16},{8,24},{1,17},{9,25},{2,18},{10,26},{3,19},{11,27},{4,20},{... | collective-permute-start | bytes 196616 | tf_op jit(solution)/shard_map/ppermute | solution.py:437
  69.2 2.5 %collective-permute-start.12 = (f32[16,1024]{1,0:T(8,128)S(1)}, f32[16,1024]{1,0:T(8,128)S(1)}, u32[]{:S(2)}, u32[]{:S(2)}) collective-permute-start(f32[16,1024]{1,0:T(8,128)S(1)} %get-tuple-element.39), channel_id=1, source_target_pairs={{0,8},{8,16},{16,24},{1,9},{9,17},{17,25},{2,10},{10,18},{18,26},{... | collective-permute-start | bytes 196616 | tf_op jit(solution)/shard_map/ppermute | solution.py:437
  71.7 17.1 %cross.1.refs_0_ = f32[136,128]{1,0:T(8,128)S(1)} custom-call(bf16[512,1024]{1,0:T(8,128)(2,1)S(1)} %get-tuple-element.37.refs_4_.grad_z, bf16[512,1024]{1,0:T(8,128)(2,1)S(1)} %copy-done.2, bf16[512,1024]{1,0:T(8,128)(2,1)S(1)} %copy-done.3, bf16[128,1024]{1,0:T(8,128)(2,1)S(1)} %collective-permute-done.refs_3_.edge, bf16[512,1024]{1,0:T(8,128)(2,1)S(1)} %copy-done.1, ...), custom_call_target="tpu_custom_call" | custom-call | tf_op jit(solution)/shard_map/cross/pallas_call | solution.py:552
  89.4 3.7 %collective-permute-start.15 = (f32[136,128]{1,0:T(8,128)S(1)}, f32[136,128]{1,0:T(8,128)S(1)}, u32[]{:S(2)}, u32[]{:S(2)}) collective-permute-start(f32[136,128]{1,0:T(8,128)S(1)} %join.1.refs_1_), channel_id=1, source_target_pairs={{0,24},{8,0},{16,8},{24,16},{1,25},{9,1},{17,9},{25,17},{2,26},{10... | collective-permute-start | bytes 208904 | tf_op jit(solution)/shard_map/ppermute | solution.py:442
  93.1 3.0 %collective-permute-done.17.refs_4_ = f32[136,128]{1,0:T(8,128)S(1)} collective-permute-done((f32[136,128]{1,0:T(8,128)S(1)}, f32[136,128]{1,0:T(8,128)S(1)}, u32[]{:S(2)}, u32[]{:S(2)}) %collective-permute-start.17) | collective-permute-done | bytes 69664 | tf_op jit(solution)/shard_map/ppermute | solution.py:442
  96.2 1.8 %collective-permute-done.16.refs_3_ = f32[136,128]{1,0:T(8,128)S(1)} collective-permute-done((f32[136,128]{1,0:T(8,128)S(1)}, f32[136,128]{1,0:T(8,128)S(1)}, u32[]{:S(2)}, u32[]{:S(2)}) %collective-permute-start.16) | collective-permute-done | bytes 69664 | tf_op jit(solution)/shard_map/ppermute | solution.py:442
  99.4 1.5 %copy.19 = f32[128,64]{0,1:T(8,128)} copy(f32[128,64]{1,0:T(8,128)} %copy-done.25) | data formatting | bytes 65536
  106.8 15.4 %last.1 = (bf16[512,1024]{1,0:T(8,128)(2,1)}, bf16[512,1024]{1,0:T(8,128)(2,1)}, bf16[512,1024]{1,0:T(8,128)(2,1)}) custom-call(bf16[512,1024]{1,0:T(8,128)(2,1)S(1)} %copy-done.8, bf16[512,1024]{1,0:T(8,128)(2,1)S(1)} %copy-done.1, f32[64,512]{1,0:T(8,128)S(1)} %copy-done.22, f32[64,512]{1,0:T(8,128)S(1)} %get-tuple-element.28.refs_4_.refs_3_, ...), custom_call_target="tpu_custom_call" | custom-call | tf_op jit(solution)/shard_map/last/pallas_call | solution.py:576
  (77 shorter events, 15.3 us)
Async XLA Ops:
  1.7 26.1 %collective-permute-start = (bf16[128,1024]{1,0:T(8,128)(2,1)S(1)}, bf16[128,1024]{1,0:T(8,128)(2,1)S(1)}, u32[]{:S(2)}, u32[]{:S(2)}) collective-permute-start(bf16[128,1024]{1,0:T(8,128)(2,1)S(1)} %multiply_convert_fusion), channel_id=1, source_target_pairs={{0,8},{8,16},{16,24},{1,9},{9,17},{17,25},{2,10},{10,18},{18,26},{... | collective-permute-start | bytes 786440 | tf_op jit(solution)/shard_map/ppermute | solution.py:437
  14.3 12.2 %copy-start.21 = (f32[64,512]{1,0:T(8,128)}, f32[64,512]{1,0:T(8,128)S(1)}, u32[]{:S(2)}) copy-start(f32[64,512]{1,0:T(8,128)S(1)} %get-tuple-element.36.refs_2_) | copy-start | bytes 393220
  14.3 13.5 %collective-permute-start.3 = (f32[16,1024]{1,0:T(8,128)S(1)}, f32[16,1024]{1,0:T(8,128)S(1)}, u32[]{:S(2)}, u32[]{:S(2)}) collective-permute-start(f32[16,1024]{1,0:T(8,128)S(1)} %get-tuple-element.30.refs_1_), channel_id=1, source_target_pairs={{24,0},{25,1},{26,2},{27,3},{28,4},{29,5},{30,6},{31,7}} | collective-permute-start | bytes 196616 | tf_op jit(solution)/shard_map/ppermute | solution.py:437
  15.6 12.2 %collective-permute-start.2 = (f32[16,1024]{1,0:T(8,128)S(1)}, f32[16,1024]{1,0:T(8,128)S(1)}, u32[]{:S(2)}, u32[]{:S(2)}) collective-permute-start(f32[16,1024]{1,0:T(8,128)S(1)} %get-tuple-element.30.refs_1_), channel_id=1, source_target_pairs={{16,0},{24,8},{17,1},{25,9},{18,2},{26,10},{19,3},{27,11},{20,4},{... | collective-permute-start | bytes 196616 | tf_op jit(solution)/shard_map/ppermute | solution.py:437
  16.9 10.9 %collective-permute-start.1 = (f32[16,1024]{1,0:T(8,128)S(1)}, f32[16,1024]{1,0:T(8,128)S(1)}, u32[]{:S(2)}, u32[]{:S(2)}) collective-permute-start(f32[16,1024]{1,0:T(8,128)S(1)} %get-tuple-element.30.refs_1_), channel_id=1, source_target_pairs={{8,0},{16,8},{24,16},{9,1},{17,9},{25,17},{10,2},{18,10},{26,18},{... | collective-permute-start | bytes 196616 | tf_op jit(solution)/shard_map/ppermute | solution.py:437
  39.0 4.5 %collective-permute-start.10 = (f32[8,512]{1,0:T(8,128)S(1)}, f32[8,512]{1,0:T(8,128)S(1)}, u32[]{:S(2)}, u32[]{:S(2)}) collective-permute-start(f32[8,512]{1,0:T(8,128)S(1)} %get-tuple-element.33.refs_6_), channel_id=1, source_target_pairs={{0,1},{1,2},{2,3},{3,4},{4,5},{5,6},{6,7},{7,0},{8,9},{9,10},{10,1... | collective-permute-start | bytes 49160 | tf_op jit(solution)/shard_map/ppermute | solution.py:442
  39.0 6.0 %collective-permute-start.9 = (f32[8,512]{1,0:T(8,128)S(1)}, f32[8,512]{1,0:T(8,128)S(1)}, u32[]{:S(2)}, u32[]{:S(2)}) collective-permute-start(f32[8,512]{1,0:T(8,128)S(1)} %get-tuple-element.33.refs_6_), channel_id=1, source_target_pairs={{0,2},{1,3},{2,4},{3,5},{4,6},{5,7},{6,0},{7,1},{8,10},{9,11},{10,... | collective-permute-start | bytes 49160 | tf_op jit(solution)/shard_map/ppermute | solution.py:442
  40.5 6.8 %collective-permute-start.8 = (f32[8,512]{1,0:T(8,128)S(1)}, f32[8,512]{1,0:T(8,128)S(1)}, u32[]{:S(2)}, u32[]{:S(2)}) collective-permute-start(f32[8,512]{1,0:T(8,128)S(1)} %get-tuple-element.33.refs_6_), channel_id=1, source_target_pairs={{0,3},{1,4},{2,5},{3,6},{4,7},{5,0},{6,1},{7,2},{8,11},{9,12},{10,... | collective-permute-start | bytes 49160 | tf_op jit(solution)/shard_map/ppermute | solution.py:442
  42.9 4.4 %collective-permute-start.7 = (f32[8,512]{1,0:T(8,128)S(1)}, f32[8,512]{1,0:T(8,128)S(1)}, u32[]{:S(2)}, u32[]{:S(2)}) collective-permute-start(f32[8,512]{1,0:T(8,128)S(1)} %get-tuple-element.33.refs_6_), channel_id=1, source_target_pairs={{0,4},{1,5},{2,6},{3,7},{4,0},{5,1},{6,2},{7,3},{8,12},{9,13},{10,... | collective-permute-start | bytes 49160 | tf_op jit(solution)/shard_map/ppermute | solution.py:442
  43.4 3.9 %collective-permute-start.6 = (f32[8,512]{1,0:T(8,128)S(1)}, f32[8,512]{1,0:T(8,128)S(1)}, u32[]{:S(2)}, u32[]{:S(2)}) collective-permute-start(f32[8,512]{1,0:T(8,128)S(1)} %get-tuple-element.33.refs_6_), channel_id=1, source_target_pairs={{0,5},{1,6},{2,7},{3,0},{4,1},{5,2},{6,3},{7,4},{8,13},{9,14},{10,... | collective-permute-start | bytes 49160 | tf_op jit(solution)/shard_map/ppermute | solution.py:442
  43.5 3.8 %collective-permute-start.5 = (f32[8,512]{1,0:T(8,128)S(1)}, f32[8,512]{1,0:T(8,128)S(1)}, u32[]{:S(2)}, u32[]{:S(2)}) collective-permute-start(f32[8,512]{1,0:T(8,128)S(1)} %get-tuple-element.33.refs_6_), channel_id=1, source_target_pairs={{0,6},{1,7},{2,0},{3,1},{4,2},{5,3},{6,4},{7,5},{8,14},{9,15},{10,... | collective-permute-start | bytes 49160 | tf_op jit(solution)/shard_map/ppermute | solution.py:442
  44.9 3.8 %collective-permute-start.4 = (f32[8,512]{1,0:T(8,128)S(1)}, f32[8,512]{1,0:T(8,128)S(1)}, u32[]{:S(2)}, u32[]{:S(2)}) collective-permute-start(f32[8,512]{1,0:T(8,128)S(1)} %get-tuple-element.33.refs_6_), channel_id=1, source_target_pairs={{0,7},{1,0},{2,1},{3,2},{4,3},{5,4},{6,5},{7,6},{8,15},{9,8},{10,9... | collective-permute-start | bytes 49160 | tf_op jit(solution)/shard_map/ppermute | solution.py:442
  48.7 23.0 %copy-start.1 = (bf16[512,1024]{1,0:T(8,128)(2,1)S(1)}, bf16[512,1024]{1,0:T(8,128)(2,1)}, u32[]{:S(2)}) copy-start(bf16[512,1024]{1,0:T(8,128)(2,1)} %cot.5) | copy-start | bytes 3145732
  48.7 23.0 %copy-start.5 = (bf16[512,1024]{1,0:T(8,128)(2,1)S(1)}, bf16[512,1024]{1,0:T(8,128)(2,1)}, u32[]{:S(2)}) copy-start(bf16[512,1024]{1,0:T(8,128)(2,1)} %q_lr.5) | copy-start | bytes 3145732
  57.8 31.0 %copy-start.9 = (bf16[512,1024]{1,0:T(8,128)(2,1)}, bf16[512,1024]{1,0:T(8,128)(2,1)S(1)}, u32[]{:S(2)}) copy-start(bf16[512,1024]{1,0:T(8,128)(2,1)S(1)} %get-tuple-element.37.refs_4_.grad_z) | copy-start | bytes 3145732
  57.8 43.2 %collective-permute-start.11 = (bf16[128,1024]{1,0:T(8,128)(2,1)}, bf16[128,1024]{1,0:T(8,128)(2,1)}, u32[]{:S(2)}, u32[]{:S(2)}) collective-permute-start(bf16[128,1024]{1,0:T(8,128)(2,1)} %get-tuple-element.38), channel_id=1, source_target_pairs={{8,0},{16,8},{24,16},{9,1},{17,9},{25,17},{10,2},{18,10},{26,18},{... | collective-permute-start | bytes 786440 | tf_op jit(solution)/shard_map/ppermute | solution.py:437
  59.1 29.8 %collective-permute-start.14 = (f32[16,1024]{1,0:T(8,128)S(1)}, f32[16,1024]{1,0:T(8,128)S(1)}, u32[]{:S(2)}, u32[]{:S(2)}) collective-permute-start(f32[16,1024]{1,0:T(8,128)S(1)} %get-tuple-element.39), channel_id=1, source_target_pairs={{0,24},{1,25},{2,26},{3,27},{4,28},{5,29},{6,30},{7,31}} | collective-permute-start | bytes 196616 | tf_op jit(solution)/shard_map/ppermute | solution.py:437
  67.9 20.9 %collective-permute-start.13 = (f32[16,1024]{1,0:T(8,128)S(1)}, f32[16,1024]{1,0:T(8,128)S(1)}, u32[]{:S(2)}, u32[]{:S(2)}) collective-permute-start(f32[16,1024]{1,0:T(8,128)S(1)} %get-tuple-element.39), channel_id=1, source_target_pairs={{0,16},{8,24},{1,17},{9,25},{2,18},{10,26},{3,19},{11,27},{4,20},{... | collective-permute-start | bytes 196616 | tf_op jit(solution)/shard_map/ppermute | solution.py:437
  69.2 19.6 %collective-permute-start.12 = (f32[16,1024]{1,0:T(8,128)S(1)}, f32[16,1024]{1,0:T(8,128)S(1)}, u32[]{:S(2)}, u32[]{:S(2)}) collective-permute-start(f32[16,1024]{1,0:T(8,128)S(1)} %get-tuple-element.39), channel_id=1, source_target_pairs={{0,8},{8,16},{16,24},{1,9},{9,17},{17,25},{2,10},{10,18},{18,26},{... | collective-permute-start | bytes 196616 | tf_op jit(solution)/shard_map/ppermute | solution.py:437
  71.7 29.2 %copy-start.24 = (f32[16,64]{1,0:T(8,128)S(1)}, f32[16,64]{1,0:T(8,128)}, u32[]{:S(2)}) copy-start(f32[16,64]{1,0:T(8,128)} %refs_9_.3) | copy-start | bytes 12292
  88.8 9.9 %copy-start.15 = (f32[16,1024]{1,0:T(8,128)}, f32[16,1024]{1,0:T(8,128)S(1)}, u32[]{:S(2)}) copy-start(f32[16,1024]{1,0:T(8,128)S(1)} %collective-permute-done.14.refs_12_.refs_5_) | copy-start | bytes 196612
  89.2 6.9 %collective-permute-start.17 = (f32[136,128]{1,0:T(8,128)S(1)}, f32[136,128]{1,0:T(8,128)S(1)}, u32[]{:S(2)}, u32[]{:S(2)}) collective-permute-start(f32[136,128]{1,0:T(8,128)S(1)} %join.1.refs_1_), channel_id=1, source_target_pairs={{0,8},{8,16},{16,24},{24,0},{1,9},{9,17},{17,25},{25,1},{2,10},{10... | collective-permute-start | bytes 208904 | tf_op jit(solution)/shard_map/ppermute | solution.py:442
  89.3 8.6 %collective-permute-start.16 = (f32[136,128]{1,0:T(8,128)S(1)}, f32[136,128]{1,0:T(8,128)S(1)}, u32[]{:S(2)}, u32[]{:S(2)}) collective-permute-start(f32[136,128]{1,0:T(8,128)S(1)} %join.1.refs_1_), channel_id=1, source_target_pairs={{0,16},{8,24},{16,0},{24,8},{1,17},{9,25},{17,1},{25,9},{2,18},{10... | collective-permute-start | bytes 208904 | tf_op jit(solution)/shard_map/ppermute | solution.py:442
  89.4 8.6 %collective-permute-start.15 = (f32[136,128]{1,0:T(8,128)S(1)}, f32[136,128]{1,0:T(8,128)S(1)}, u32[]{:S(2)}, u32[]{:S(2)}) collective-permute-start(f32[136,128]{1,0:T(8,128)S(1)} %join.1.refs_1_), channel_id=1, source_target_pairs={{0,24},{8,0},{16,8},{24,16},{1,25},{9,1},{17,9},{25,17},{2,26},{10... | collective-permute-start | bytes 208904 | tf_op jit(solution)/shard_map/ppermute | solution.py:442
  (21 other events, 88.5 us)
where the time goes:
time: 123 us; the launch traced here: 122 us
  Pallas kernels  64 us (52%)
  starting transfers between devices  34.9 us (28%)
  local copies, waits for them, and re-layouts  15.1 us (12%)
  waiting for transfers between devices  6.27 us (5%)
    ppermute x8, starting transfers between devices, shifted(): lax.ppermute(value, axis, [(source, source + steps) for source in range(f...  22.7 us
    pallas_call x1, Pallas kernels, shards(): pl.pallas_call(functools.partial(cross_kernel, width), grid=(steps,), in_...  17.1 us
    pallas_call x1, Pallas kernels, shards(): pl.pallas_call(functools.partial(last_kernel, width, peers), grid=(steps,...  15.4 us
    unnamed x56, local copies, waits for them, and re-layouts  15.1 us
    ppermute x10, starting transfers between devices, rotated(): lax.ppermute(value, axis, [(source, (source - steps) % count) for source...  12.1 us
    pallas_call x1, Pallas kernels, shards(): pl.pallas_call(functools.partial(medium_kernel, width, peers), grid=(step...  11.1 us
    pallas_call x1, Pallas kernels, shards(): pl.pallas_call(functools.partial(back_kernel, width, taps), grid=(steps,)...  8.17 us
    pallas_call x1, Pallas kernels, shards(): pl.pallas_call(functools.partial(norm_kernel, width, float(chans * chan_c...  8.12 us
  transfers between devices with their start and end apart: 18, of which 3 were waited for; matrix products, arithmetic and copies ran while one was open for 2% of the time, Pallas kernels for 24%

commit v1 on v0

--- a/solution.py
+++ b/solution.py
@@ -11,7 +11,7 @@
 LANES = 128
 F32 = jnp.float32
 BF16 = jnp.bfloat16
-VMEM_LIMIT = 48 * 1024 * 1024
+VMEM_LIMIT = 24 * 1024 * 1024
 
 
 def iota(shape, dim):
@@ -86,9 +86,9 @@
 
 
 def carry(received, rates_c, rows):
-    total = received[0]
+    total = received[0].astype(F32)
     for k in range(1, len(received)):
-        total = total + jnp.exp(rates_c * (-float(rows * k))) * received[k]
+        total = total + jnp.exp(rates_c * (-float(rows * k))) * received[k].astype(F32)
     return total
 
 
@@ -125,7 +125,7 @@
     column = pick_column(rates, first, width)
     powers = jnp.exp(-column * iota((LANES, rows), 1).astype(F32)).astype(BF16)
     grad = (cot[...].astype(F32) * q_lr[...].astype(F32)).astype(BF16)
-    states[...] = fold_states(powers, grad, modes, width)
+    states[...] = fold_states(powers, grad, modes, width).astype(BF16)
     forward = iota((count, rows), 1)
     backward = rows - taps - forward
     backward = jnp.where(backward < 0, backward + rows, backward)
@@ -274,7 +274,8 @@
     grad_edge[...] = grad_conv[0:taps]
     column = pick_column(rates, i * (LANES // width), width)
     reach = (rows - 1 - iota((LANES, rows), 1)).astype(F32)
-    states[...] = fold_states(jnp.exp(-column * reach).astype(BF16), w_lr, modes, width)
+    found = fold_states(jnp.exp(-column * reach).astype(BF16), w_lr, modes, width)
+    states[...] = found.astype(BF16)
 
 
 def cross_kernel(
@@ -332,27 +333,29 @@
 def join_kernel(width, rows, peers, *refs):
     pack, states, rates_ref = refs[:3]
     received = refs[3 : 3 + peers]
-    out = refs[3 + peers]
+    out, total = refs[3 + peers :]
     rates = rates_ref[...]
     modes, groups = rates.shape
     count = LANES // width
-    out[...] = pack[...]
+    total[...] = pack[...]
     for i in range(groups // count):
         part = slice(i * LANES, (i + 1) * LANES)
         rates_c = pick_channels(rates, i * count, width)
         carried = carry([r[:, part] for r in received], rates_c, rows)
-        product = jnp.exp(-rates_c) * carried * states[:, part]
+        product = jnp.exp(-rates_c) * carried * states[:, part].astype(F32)
         shape = (LANES, LANES)
         member = jnp.where(iota((count, LANES), 1) // width == iota((count, LANES), 0), 1.0, 0.0)
         padded = jnp.concatenate([product, jnp.zeros((LANES - modes, LANES), F32)], axis=0)
         at = groups + i * count
-        out[at : at + count, :] += dot_t(member, padded, lax.Precision.HIGHEST)
+        total[at : at + count, :] += dot_t(member, padded, lax.Precision.HIGHEST)
+    out[...] = total[...].astype(BF16)
 
 
 def last_kernel(width, peers, *refs):
     (w, cot, hr, taps_rows, grad_z, after, k, v, rates_ref, res_ref) = refs[:10]
     received = refs[10 : 10 + peers]
-    grad_q, grad_k, grad_v, near, far, data, table, wide = refs[10 + peers :]
+    grad_q, grad_k, grad_v, mark, near, far, data, table, wide = refs[10 + peers :]
+    mark[...] = jnp.zeros_like(mark)
     i = pl.program_id(0)
     rows = w.shape[0]
     taps = after.shape[0]
@@ -408,8 +411,8 @@
 
 def close_kernel(sharers, norm_terms, gain_terms, *refs):
     rates_ref = refs[0]
-    packs = [r[...] for r in refs[1 : 1 + sharers]]
-    taps_out, modes_out, gain_out = refs[1 + sharers :]
+    packs = [r[...].astype(F32) for r in refs[1 : 1 + sharers]]
+    taps_out, modes_out, gain_out = refs[2 + sharers :]
     while len(packs) > 1:
         half = len(packs) // 2
         if len(packs) % 2:
@@ -475,8 +478,12 @@
 
     key_edge = (k_mr[rows - taps :].astype(F32) * v_mr[rows - taps :].astype(F32)).astype(BF16)
     edge = shifted(key_edge, "seq", 1)
-
-    small = shape((modes, chans), F32)
+    q_mr, k_mr, v_mr, q_lr, k_lr, cotangent = [
+        pltpu.with_memory_space_constraint(x, pltpu.HBM)
+        for x in (q_mr, k_mr, v_mr, q_lr, k_lr, cotangent)
+    ]
+
+    small = shape((modes, chans), BF16)
     back_states, h, hr, taps_rows = pl.pallas_call(
         functools.partial(prep_kernel, width),
         grid=(steps,),
@@ -567,20 +574,21 @@
 
     pack = pl.pallas_call(
         functools.partial(join_kernel, width, rows, peers),
-        out_shape=shape(pack_shape, F32),
+        out_shape=shape(pack_shape, BF16),
+        scratch_shapes=[pltpu.VMEM(pack_shape, F32)],
         compiler_params=pltpu.CompilerParams(vmem_limit_bytes=VMEM_LIMIT),
         name="join",
     )(pack, back_states, decay_rates, *from_earlier)
     packs = [pack] + [rotated(pack, "seq", k) for k in range(1, seq_count)]
 
-    grad_q_lr, grad_k_mr, grad_v_mr = pl.pallas_call(
+    grad_q_lr, grad_k_mr, grad_v_mr, mark = pl.pallas_call(
         functools.partial(last_kernel, width, peers),
         grid=(steps,),
         in_specs=[wide, wide, h_spec, down, wide, edge_spec, wide, wide]
         + [whole(decay_rates), whole(residues)]
         + [state_spec] * peers,
-        out_specs=[wide, wide, wide],
-        out_shape=[shape((rows, chans), BF16)] * 3,
+        out_specs=[wide, wide, wide, pl.BlockSpec((8, LANES), lambda i: (0, 0))],
+        out_shape=[shape((rows, chans), BF16)] * 3 + [shape((8, LANES), F32)],
         scratch_shapes=[
             pltpu.VMEM((half, count * half), BF16),
             pltpu.VMEM((half, count * half), BF16),
@@ -592,15 +600,17 @@
         name="last",
     )(w, cotangent, hr, taps_rows, grad_z, after, k_mr, v_mr, decay_rates, residues, *from_earlier)
 
+    in_vmem = pl.BlockSpec(memory_space=pltpu.VMEM)
     total_rows = rows * seq_count
     taps_sum, mode_sum, gain_sum = pl.pallas_call(
         functools.partial(
             close_kernel, seq_count, float(total_rows * width) ** 0.5, float(total_rows) ** 0.5
         ),
+        in_specs=[in_vmem] * (1 + seq_count) + [in_vmem],
         out_shape=[shape((taps, groups), F32), shape((modes, groups), F32), shape((steps, LANES), F32)],
         compiler_params=pltpu.CompilerParams(vmem_limit_bytes=VMEM_LIMIT),
         name="close",
-    )(decay_rates, *packs)
+    )(decay_rates, *packs, mark)
     return (
         grad_q_mr,
         grad_k_mr,

time: 123 us -> 106 us (0.86)
  local copies, waits for them, and re-layouts: 15.1 us -> 2.94 us
  waiting for transfers between devices: 6.27 us -> 1.47 us
    unnamed x56 -> x12, local copies, waits for them, and re-layouts: 15.1 us -> 2.94 us
    ppermute x10, waiting for transfers between devices: 6.25 us -> 1.44 us  [rotated(): lax.ppermute(value, axis, [(source, (source - steps) % count) for source...]
    pallas_call x1, Pallas kernels: 2.94 us -> 5.54 us  [shards(): pl.pallas_call(functools.partial(prep_kernel, width), grid=(steps,), in_s...]
  transfers between devices with their start and end apart: 18 -> 18, of which waited for: 3 -> 1; matrix products, arithmetic and copies ran while one was open for 2% -> 1% of each run, Pallas kernels for 24% -> 44%
where the time goes in v1:
time: 106 us; the launch traced here: 105 us
  Pallas kernels  64.6 us (61%)
  starting transfers between devices  34.2 us (32%)
  local copies, waits for them, and re-layouts  2.94 us (3%)
  waiting for transfers between devices  1.47 us (1%)
  other arithmetic  1.1 us (1%)
    ppermute x8, starting transfers between devices, shifted(): lax.ppermute(value, axis, [(source, source + steps) for source in range(f...  22 us
    pallas_call x1, Pallas kernels, shards(): pl.pallas_call(functools.partial(cross_kernel, width), grid=(steps,), in_...  16.6 us
    pallas_call x1, Pallas kernels, shards(): pl.pallas_call(functools.partial(last_kernel, width, peers), grid=(steps,...  15 us
    ppermute x10, starting transfers between devices, rotated(): lax.ppermute(value, axis, [(source, (source - steps) % count) for source...  12.2 us
    pallas_call x1, Pallas kernels, shards(): pl.pallas_call(functools.partial(medium_kernel, width, peers), grid=(step...  10.1 us
    pallas_call x1, Pallas kernels, shards(): pl.pallas_call(functools.partial(back_kernel, width, taps), grid=(steps,)...  8.64 us
    pallas_call x1, Pallas kernels, shards(): pl.pallas_call(functools.partial(norm_kernel, width, float(chans * chan_c...  7.55 us
    pallas_call x1, Pallas kernels, shards(): pl.pallas_call(functools.partial(prep_kernel, width), grid=(steps,), in_s...  5.54 us
  transfers between devices with their start and end apart: 18, of which 1 were waited for; matrix products, arithmetic and copies ran while one was open for 1% of the time, Pallas kernels for 44%

profile of v1, /device:TPU:0, one launch (start us, length us, event | category | flops | bytes accessed | tf_op | source)
XLA Modules:
  0.0 105.2 jit_solution(1728002382477884000)
XLA Ops:
  0.6 1.1 %multiply_convert_fusion = bf16[128,1024]{1,0:T(8,128)(2,1)S(1)} fusion(bf16[512,1024]{1,0:T(8,128)(2,1)} %v.1, bf16[512,1024]{1,0:T(8,128)(2,1)} %k.1), kind=kLoop, calls=%fused_computation | loop fusion | flops 524288 | bytes 786432 | tf_op jit(solution)/shard_map/convert_element_type | solution.py:479
  1.7 4.9 %collective-permute-start = (bf16[128,1024]{1,0:T(8,128)(2,1)S(1)}, bf16[128,1024]{1,0:T(8,128)(2,1)S(1)}, u32[]{:S(2)}, u32[]{:S(2)}) collective-permute-start(bf16[128,1024]{1,0:T(8,128)(2,1)S(1)} %multiply_convert_fusion), channel_id=1, source_target_pairs={{0,8},{8,16},{16,24},{1,9},{9,17},{17,25},{2,10},{10,18},{18,26},{... | collective-permute-start | bytes 786440 | tf_op jit(solution)/shard_map/ppermute | solution.py:440
  6.7 0.8 copy.18.filt
  8.9 5.5 %prep.1 = (bf16[16,1024]{1,0:T(8,128)(2,1)S(1)}, f32[64,512]{1,0:T(8,128)S(1)}, f32[64,512]{1,0:T(8,128)S(1)}, f32[64,512]{1,0:T(8,128)S(1)}) custom-call(bf16[512,1024]{1,0:T(8,128)(2,1)} %cot.5, bf16[512,1024]{1,0:T(8,128)(2,1)} %q_lr.5, f32[16,64]{1,0:T(8,128)S(1)} %copy-done, f32[16,64]{1,0:T(8,128)S(1)} %copy-done.2, bf16[128,64]{1,0:T(8,128)(2,1)S(1)} %copy.18.filt), custom_call_target="tpu_custom_call" | custom-call | tf_op jit(solution)/shard_map/prep/pallas_call | solution.py:487
  14.5 1.3 %collective-permute-start.3 = (bf16[16,1024]{1,0:T(8,128)(2,1)S(1)}, bf16[16,1024]{1,0:T(8,128)(2,1)S(1)}, u32[]{:S(2)}, u32[]{:S(2)}) collective-permute-start(bf16[16,1024]{1,0:T(8,128)(2,1)S(1)} %get-tuple-element.31.refs_1_), channel_id=1, source_target_pairs={{24,0},{25,1},{26,2},{27,3},{28,4},{29,5},{30,6},{31,7}} | collective-permute-start | bytes 98312 | tf_op jit(solution)/shard_map/ppermute | solution.py:440
  15.8 1.3 %collective-permute-start.2 = (bf16[16,1024]{1,0:T(8,128)(2,1)S(1)}, bf16[16,1024]{1,0:T(8,128)(2,1)S(1)}, u32[]{:S(2)}, u32[]{:S(2)}) collective-permute-start(bf16[16,1024]{1,0:T(8,128)(2,1)S(1)} %get-tuple-element.31.refs_1_), channel_id=1, source_target_pairs={{16,0},{24,8},{17,1},{25,9},{18,2},{26,10},{19,3},{27,11},{20,4},{... | collective-permute-start | bytes 98312 | tf_op jit(solution)/shard_map/ppermute | solution.py:440
  17.1 1.3 %collective-permute-start.1 = (bf16[16,1024]{1,0:T(8,128)(2,1)S(1)}, bf16[16,1024]{1,0:T(8,128)(2,1)S(1)}, u32[]{:S(2)}, u32[]{:S(2)}) collective-permute-start(bf16[16,1024]{1,0:T(8,128)(2,1)S(1)} %get-tuple-element.31.refs_1_), channel_id=1, source_target_pairs={{8,0},{16,8},{24,16},{9,1},{17,9},{25,17},{10,2},{18,10},{26,18},{... | collective-permute-start | bytes 98312 | tf_op jit(solution)/shard_map/ppermute | solution.py:440
  18.4 8.6 %back.1.refs_5_ = f32[512,1024]{1,0:T(8,128)S(1)} custom-call(bf16[512,1024]{1,0:T(8,128)(2,1)} %cot.5, bf16[512,1024]{1,0:T(8,128)(2,1)} %q_lr.5, f32[64,512]{1,0:T(8,128)S(1)} %get-tuple-element.30.h), custom_call_target="tpu_custom_call" | custom-call | tf_op jit(solution)/shard_map/back/pallas_call | solution.py:503
  27.1 10.1 %medium.1 = (f32[512,1024]{1,0:T(8,128)S(1)}, f32[512,1024]{1,0:T(8,128)S(1)}, f32[8,512]{1,0:T(8,128)S(1)}) custom-call(bf16[512,1024]{1,0:T(8,128)(2,1)} %refs_0_.4, bf16[512,1024]{1,0:T(8,128)(2,1)} %k.1, bf16[512,1024]{1,0:T(8,128)(2,1)} %v.1, bf16[128,1024]{1,0:T(8,128)(2,1)S(1)} %collective-permute-done.refs_3_.edge, ...), custom_call_target="tpu_custom_call" | custom-call | tf_op jit(solution)/shard_map/medium/pallas_call | solution.py:518
  37.3 1.5 %collective-permute-start.9 = (f32[8,512]{1,0:T(8,128)S(1)}, f32[8,512]{1,0:T(8,128)S(1)}, u32[]{:S(2)}, u32[]{:S(2)}) collective-permute-start(f32[8,512]{1,0:T(8,128)S(1)} %get-tuple-element.34.refs_6_), channel_id=1, source_target_pairs={{0,2},{1,3},{2,4},{3,5},{4,6},{5,7},{6,0},{7,1},{8,10},{9,11},{10,... | collective-permute-start | bytes 49160 | tf_op jit(solution)/shard_map/ppermute | solution.py:445
  38.8 2.4 %collective-permute-start.8 = (f32[8,512]{1,0:T(8,128)S(1)}, f32[8,512]{1,0:T(8,128)S(1)}, u32[]{:S(2)}, u32[]{:S(2)}) collective-permute-start(f32[8,512]{1,0:T(8,128)S(1)} %get-tuple-element.34.refs_6_), channel_id=1, source_target_pairs={{0,3},{1,4},{2,5},{3,6},{4,7},{5,0},{6,1},{7,2},{8,11},{9,12},{10,... | collective-permute-start | bytes 49160 | tf_op jit(solution)/shard_map/ppermute | solution.py:445
  41.8 1.4 %collective-permute-start.5 = (f32[8,512]{1,0:T(8,128)S(1)}, f32[8,512]{1,0:T(8,128)S(1)}, u32[]{:S(2)}, u32[]{:S(2)}) collective-permute-start(f32[8,512]{1,0:T(8,128)S(1)} %get-tuple-element.34.refs_6_), channel_id=1, source_target_pairs={{0,6},{1,7},{2,0},{3,1},{4,2},{5,3},{6,4},{7,5},{8,14},{9,15},{10,... | collective-permute-start | bytes 49160 | tf_op jit(solution)/shard_map/ppermute | solution.py:445
  43.3 2.3 %collective-permute-start.4 = (f32[8,512]{1,0:T(8,128)S(1)}, f32[8,512]{1,0:T(8,128)S(1)}, u32[]{:S(2)}, u32[]{:S(2)}) collective-permute-start(f32[8,512]{1,0:T(8,128)S(1)} %get-tuple-element.34.refs_6_), channel_id=1, source_target_pairs={{0,7},{1,0},{2,1},{3,2},{4,3},{5,4},{6,5},{7,6},{8,15},{9,8},{10,9... | collective-permute-start | bytes 49160 | tf_op jit(solution)/shard_map/ppermute | solution.py:445
  45.6 1.4 %collective-permute-done.4.refs_7_ = f32[8,512]{1,0:T(8,128)S(1)} collective-permute-done((f32[8,512]{1,0:T(8,128)S(1)}, f32[8,512]{1,0:T(8,128)S(1)}, u32[]{:S(2)}, u32[]{:S(2)}) %collective-permute-start.4) | collective-permute-done | bytes 16416 | tf_op jit(solution)/shard_map/ppermute | solution.py:445
  47.0 7.5 %norm.1 = (bf16[512,1024]{1,0:T(8,128)(2,1)S(1)}, bf16[512,1024]{1,0:T(8,128)(2,1)S(1)}, bf16[128,1024]{1,0:T(8,128)(2,1)S(1)}, bf16[512,1024]{1,0:T(8,128)(2,1)...) custom-call(bf16[512,1024]{1,0:T(8,128)(2,1)} %refs_0_.4, ...), custom_call_target="tpu_custom_call" | custom-call | tf_op jit(solution)/shard_map/norm/pallas_call | solution.py:537
  54.6 1.3 %collective-permute-start.11 = (bf16[128,1024]{1,0:T(8,128)(2,1)S(1)}, bf16[128,1024]{1,0:T(8,128)(2,1)S(1)}, u32[]{:S(2)}, u32[]{:S(2)}) collective-permute-start(bf16[128,1024]{1,0:T(8,128)(2,1)S(1)} %get-tuple-element.39), channel_id=1, source_target_pairs={{8,0},{16,8},{24,16},{9,1},{17,9},{25,17},{10,2},{18,10},{26,18},{... | collective-permute-start | bytes 786440 | tf_op jit(solution)/shard_map/ppermute | solution.py:440
  55.8 8.2 %collective-permute-start.14 = (bf16[16,1024]{1,0:T(8,128)(2,1)S(1)}, bf16[16,1024]{1,0:T(8,128)(2,1)S(1)}, u32[]{:S(2)}, u32[]{:S(2)}) collective-permute-start(bf16[16,1024]{1,0:T(8,128)(2,1)S(1)} %get-tuple-element.40), channel_id=1, source_target_pairs={{0,24},{1,25},{2,26},{3,27},{4,28},{5,29},{6,30},{7,31}} | collective-permute-start | bytes 98312 | tf_op jit(solution)/shard_map/ppermute | solution.py:440
  64.0 1.3 %collective-permute-start.13 = (bf16[16,1024]{1,0:T(8,128)(2,1)S(1)}, bf16[16,1024]{1,0:T(8,128)(2,1)S(1)}, u32[]{:S(2)}, u32[]{:S(2)}) collective-permute-start(bf16[16,1024]{1,0:T(8,128)(2,1)S(1)} %get-tuple-element.40), channel_id=1, source_target_pairs={{0,16},{8,24},{1,17},{9,25},{2,18},{10,26},{3,19},{11,27},{4,20},{... | collective-permute-start | bytes 98312 | tf_op jit(solution)/shard_map/ppermute | solution.py:440
  65.3 2.5 %collective-permute-start.12 = (bf16[16,1024]{1,0:T(8,128)(2,1)S(1)}, bf16[16,1024]{1,0:T(8,128)(2,1)S(1)}, u32[]{:S(2)}, u32[]{:S(2)}) collective-permute-start(bf16[16,1024]{1,0:T(8,128)(2,1)S(1)} %get-tuple-element.40), channel_id=1, source_target_pairs={{0,8},{8,16},{16,24},{1,9},{9,17},{17,25},{2,10},{10,18},{18,26},{... | collective-permute-start | bytes 98312 | tf_op jit(solution)/shard_map/ppermute | solution.py:440
  67.8 16.6 %cross.1.refs_0_ = f32[136,128]{1,0:T(8,128)S(1)} custom-call(bf16[512,1024]{1,0:T(8,128)(2,1)S(1)} %get-tuple-element.38.refs_4_.grad_z, bf16[512,1024]{1,0:T(8,128)(2,1)} %k.1, bf16[512,1024]{1,0:T(8,128)(2,1)} %v.1, bf16[128,1024]{1,0:T(8,128)(2,1)S(1)} %collective-permute-done.refs_3_.edge, bf16[512,1024]{1,0:T(8,128)(2,1)} %cot.5, ...), custom_call_target="tpu_custom_call" | custom-call | tf_op jit(solution)/shard_map/cross/pallas_call | solution.py:559
  84.9 3.7 %collective-permute-start.15 = (bf16[136,128]{1,0:T(8,128)(2,1)S(1)}, bf16[136,128]{1,0:T(8,128)(2,1)S(1)}, u32[]{:S(2)}, u32[]{:S(2)}) collective-permute-start(bf16[136,128]{1,0:T(8,128)(2,1)S(1)} %join.1.refs_1_), channel_id=1, source_target_pairs={{0,24},{8,0},{16,8},{24,16},{1,25},{9,1},{17,9},{25,17},{2,26},{10... | collective-permute-start | bytes 104456 | tf_op jit(solution)/shard_map/ppermute | solution.py:445
  88.6 15.0 %last.1 = (bf16[512,1024]{1,0:T(8,128)(2,1)}, bf16[512,1024]{1,0:T(8,128)(2,1)}, bf16[512,1024]{1,0:T(8,128)(2,1)}, f32[8,128]{1,0:T(8,128)S(1)}) custom-call(bf16[512,1024]{1,0:T(8,128)(2,1)S(1)} %get-tuple-element.36.refs_0_.w, bf16[512,1024]{1,0:T(8,128)(2,1)} %cot.5, f32[64,512]{1,0:T(8,128)S(1)} %get-tuple-element.37.refs_2_, ...), custom_call_target="tpu_custom_call" | custom-call | tf_op jit(solution)/shard_map/last/pallas_call | solution.py:584
  103.7 0.8 close.1
  104.5 0.7 copy.19
  (33 shorter events, 2.6 us)
Async XLA Ops:
  1.7 25.3 %collective-permute-start = (bf16[128,1024]{1,0:T(8,128)(2,1)S(1)}, bf16[128,1024]{1,0:T(8,128)(2,1)S(1)}, u32[]{:S(2)}, u32[]{:S(2)}) collective-permute-start(bf16[128,1024]{1,0:T(8,128)(2,1)S(1)} %multiply_convert_fusion), channel_id=1, source_target_pairs={{0,8},{8,16},{16,24},{1,9},{9,17},{17,25},{2,10},{10,18},{18,26},{... | collective-permute-start | bytes 786440 | tf_op jit(solution)/shard_map/ppermute | solution.py:440
  7.5 0.7 copy-start
  8.2 0.7 copy-start.2
  14.5 12.6 %collective-permute-start.3 = (bf16[16,1024]{1,0:T(8,128)(2,1)S(1)}, bf16[16,1024]{1,0:T(8,128)(2,1)S(1)}, u32[]{:S(2)}, u32[]{:S(2)}) collective-permute-start(bf16[16,1024]{1,0:T(8,128)(2,1)S(1)} %get-tuple-element.31.refs_1_), channel_id=1, source_target_pairs={{24,0},{25,1},{26,2},{27,3},{28,4},{29,5},{30,6},{31,7}} | collective-permute-start | bytes 98312 | tf_op jit(solution)/shard_map/ppermute | solution.py:440
  15.8 11.3 %collective-permute-start.2 = (bf16[16,1024]{1,0:T(8,128)(2,1)S(1)}, bf16[16,1024]{1,0:T(8,128)(2,1)S(1)}, u32[]{:S(2)}, u32[]{:S(2)}) collective-permute-start(bf16[16,1024]{1,0:T(8,128)(2,1)S(1)} %get-tuple-element.31.refs_1_), channel_id=1, source_target_pairs={{16,0},{24,8},{17,1},{25,9},{18,2},{26,10},{19,3},{27,11},{20,4},{... | collective-permute-start | bytes 98312 | tf_op jit(solution)/shard_map/ppermute | solution.py:440
  17.1 10.0 %collective-permute-start.1 = (bf16[16,1024]{1,0:T(8,128)(2,1)S(1)}, bf16[16,1024]{1,0:T(8,128)(2,1)S(1)}, u32[]{:S(2)}, u32[]{:S(2)}) collective-permute-start(bf16[16,1024]{1,0:T(8,128)(2,1)S(1)} %get-tuple-element.31.refs_1_), channel_id=1, source_target_pairs={{8,0},{16,8},{24,16},{9,1},{17,9},{25,17},{10,2},{18,10},{26,18},{... | collective-permute-start | bytes 98312 | tf_op jit(solution)/shard_map/ppermute | solution.py:440
  18.4 8.7 %copy-start.1 = (f32[16,64]{1,0:T(8,128)S(1)}, f32[16,64]{1,0:T(8,128)}, u32[]{:S(2)}) copy-start(f32[16,64]{1,0:T(8,128)} %refs_0_.5) | copy-start | bytes 12292
  18.4 8.7 %copy-start.4 = (f32[1024]{0:T(1024)S(1)}, f32[1024]{0:T(1024)}, u32[]{:S(2)}) copy-start(f32[1024]{0:T(1024)} %param.19) | copy-start | bytes 12292
  37.2 4.6 %collective-permute-start.10 = (f32[8,512]{1,0:T(8,128)S(1)}, f32[8,512]{1,0:T(8,128)S(1)}, u32[]{:S(2)}, u32[]{:S(2)}) collective-permute-start(f32[8,512]{1,0:T(8,128)S(1)} %get-tuple-element.34.refs_6_), channel_id=1, source_target_pairs={{0,1},{1,2},{2,3},{3,4},{4,5},{5,6},{6,7},{7,0},{8,9},{9,10},{10,1... | collective-permute-start | bytes 49160 | tf_op jit(solution)/shard_map/ppermute | solution.py:445
  37.3 6.0 %collective-permute-start.9 = (f32[8,512]{1,0:T(8,128)S(1)}, f32[8,512]{1,0:T(8,128)S(1)}, u32[]{:S(2)}, u32[]{:S(2)}) collective-permute-start(f32[8,512]{1,0:T(8,128)S(1)} %get-tuple-element.34.refs_6_), channel_id=1, source_target_pairs={{0,2},{1,3},{2,4},{3,5},{4,6},{5,7},{6,0},{7,1},{8,10},{9,11},{10,... | collective-permute-start | bytes 49160 | tf_op jit(solution)/shard_map/ppermute | solution.py:445
  38.8 6.7 %collective-permute-start.8 = (f32[8,512]{1,0:T(8,128)S(1)}, f32[8,512]{1,0:T(8,128)S(1)}, u32[]{:S(2)}, u32[]{:S(2)}) collective-permute-start(f32[8,512]{1,0:T(8,128)S(1)} %get-tuple-element.34.refs_6_), channel_id=1, source_target_pairs={{0,3},{1,4},{2,5},{3,6},{4,7},{5,0},{6,1},{7,2},{8,11},{9,12},{10,... | collective-permute-start | bytes 49160 | tf_op jit(solution)/shard_map/ppermute | solution.py:445
  41.2 4.4 %collective-permute-start.7 = (f32[8,512]{1,0:T(8,128)S(1)}, f32[8,512]{1,0:T(8,128)S(1)}, u32[]{:S(2)}, u32[]{:S(2)}) collective-permute-start(f32[8,512]{1,0:T(8,128)S(1)} %get-tuple-element.34.refs_6_), channel_id=1, source_target_pairs={{0,4},{1,5},{2,6},{3,7},{4,0},{5,1},{6,2},{7,3},{8,12},{9,13},{10,... | collective-permute-start | bytes 49160 | tf_op jit(solution)/shard_map/ppermute | solution.py:445
  41.7 3.9 %collective-permute-start.6 = (f32[8,512]{1,0:T(8,128)S(1)}, f32[8,512]{1,0:T(8,128)S(1)}, u32[]{:S(2)}, u32[]{:S(2)}) collective-permute-start(f32[8,512]{1,0:T(8,128)S(1)} %get-tuple-element.34.refs_6_), channel_id=1, source_target_pairs={{0,5},{1,6},{2,7},{3,0},{4,1},{5,2},{6,3},{7,4},{8,13},{9,14},{10,... | collective-permute-start | bytes 49160 | tf_op jit(solution)/shard_map/ppermute | solution.py:445
  41.8 3.8 %collective-permute-start.5 = (f32[8,512]{1,0:T(8,128)S(1)}, f32[8,512]{1,0:T(8,128)S(1)}, u32[]{:S(2)}, u32[]{:S(2)}) collective-permute-start(f32[8,512]{1,0:T(8,128)S(1)} %get-tuple-element.34.refs_6_), channel_id=1, source_target_pairs={{0,6},{1,7},{2,0},{3,1},{4,2},{5,3},{6,4},{7,5},{8,14},{9,15},{10,... | collective-permute-start | bytes 49160 | tf_op jit(solution)/shard_map/ppermute | solution.py:445
  43.3 3.7 %collective-permute-start.4 = (f32[8,512]{1,0:T(8,128)S(1)}, f32[8,512]{1,0:T(8,128)S(1)}, u32[]{:S(2)}, u32[]{:S(2)}) collective-permute-start(f32[8,512]{1,0:T(8,128)S(1)} %get-tuple-element.34.refs_6_), channel_id=1, source_target_pairs={{0,7},{1,0},{2,1},{3,2},{4,3},{5,4},{6,5},{7,6},{8,15},{9,8},{10,9... | collective-permute-start | bytes 49160 | tf_op jit(solution)/shard_map/ppermute | solution.py:445
  54.6 34.1 %collective-permute-start.11 = (bf16[128,1024]{1,0:T(8,128)(2,1)S(1)}, bf16[128,1024]{1,0:T(8,128)(2,1)S(1)}, u32[]{:S(2)}, u32[]{:S(2)}) collective-permute-start(bf16[128,1024]{1,0:T(8,128)(2,1)S(1)} %get-tuple-element.39), channel_id=1, source_target_pairs={{8,0},{16,8},{24,16},{9,1},{17,9},{25,17},{10,2},{18,10},{26,18},{... | collective-permute-start | bytes 786440 | tf_op jit(solution)/shard_map/ppermute | solution.py:440
  55.8 28.5 %collective-permute-start.14 = (bf16[16,1024]{1,0:T(8,128)(2,1)S(1)}, bf16[16,1024]{1,0:T(8,128)(2,1)S(1)}, u32[]{:S(2)}, u32[]{:S(2)}) collective-permute-start(bf16[16,1024]{1,0:T(8,128)(2,1)S(1)} %get-tuple-element.40), channel_id=1, source_target_pairs={{0,24},{1,25},{2,26},{3,27},{4,28},{5,29},{6,30},{7,31}} | collective-permute-start | bytes 98312 | tf_op jit(solution)/shard_map/ppermute | solution.py:440
  64.0 20.4 %collective-permute-start.13 = (bf16[16,1024]{1,0:T(8,128)(2,1)S(1)}, bf16[16,1024]{1,0:T(8,128)(2,1)S(1)}, u32[]{:S(2)}, u32[]{:S(2)}) collective-permute-start(bf16[16,1024]{1,0:T(8,128)(2,1)S(1)} %get-tuple-element.40), channel_id=1, source_target_pairs={{0,16},{8,24},{1,17},{9,25},{2,18},{10,26},{3,19},{11,27},{4,20},{... | collective-permute-start | bytes 98312 | tf_op jit(solution)/shard_map/ppermute | solution.py:440
  65.3 19.1 %collective-permute-start.12 = (bf16[16,1024]{1,0:T(8,128)(2,1)S(1)}, bf16[16,1024]{1,0:T(8,128)(2,1)S(1)}, u32[]{:S(2)}, u32[]{:S(2)}) collective-permute-start(bf16[16,1024]{1,0:T(8,128)(2,1)S(1)} %get-tuple-element.40), channel_id=1, source_target_pairs={{0,8},{8,16},{16,24},{1,9},{9,17},{17,25},{2,10},{10,18},{18,26},{... | collective-permute-start | bytes 98312 | tf_op jit(solution)/shard_map/ppermute | solution.py:440
  67.8 20.8 %copy-start.3 = (f32[16,64]{1,0:T(8,128)S(1)}, f32[16,64]{1,0:T(8,128)}, u32[]{:S(2)}) copy-start(f32[16,64]{1,0:T(8,128)} %refs_9_.3) | copy-start | bytes 12292
  84.8 18.9 %collective-permute-start.17 = (bf16[136,128]{1,0:T(8,128)(2,1)S(1)}, bf16[136,128]{1,0:T(8,128)(2,1)S(1)}, u32[]{:S(2)}, u32[]{:S(2)}) collective-permute-start(bf16[136,128]{1,0:T(8,128)(2,1)S(1)} %join.1.refs_1_), channel_id=1, source_target_pairs={{0,8},{8,16},{16,24},{24,0},{1,9},{9,17},{17,25},{25,1},{2,10},{10... | collective-permute-start | bytes 104456 | tf_op jit(solution)/shard_map/ppermute | solution.py:445
  84.8 18.8 %collective-permute-start.16 = (bf16[136,128]{1,0:T(8,128)(2,1)S(1)}, bf16[136,128]{1,0:T(8,128)(2,1)S(1)}, u32[]{:S(2)}, u32[]{:S(2)}) collective-permute-start(bf16[136,128]{1,0:T(8,128)(2,1)S(1)} %join.1.refs_1_), channel_id=1, source_target_pairs={{0,16},{8,24},{16,0},{24,8},{1,17},{9,25},{17,1},{25,9},{2,18},{10... | collective-permute-start | bytes 104456 | tf_op jit(solution)/shard_map/ppermute | solution.py:445
  84.9 18.8 %collective-permute-start.15 = (bf16[136,128]{1,0:T(8,128)(2,1)S(1)}, bf16[136,128]{1,0:T(8,128)(2,1)S(1)}, u32[]{:S(2)}, u32[]{:S(2)}) collective-permute-start(bf16[136,128]{1,0:T(8,128)(2,1)S(1)} %join.1.refs_1_), channel_id=1, source_target_pairs={{0,24},{8,0},{16,8},{24,16},{1,25},{9,1},{17,9},{25,17},{2,26},{10... | collective-permute-start | bytes 104456 | tf_op jit(solution)/shard_map/ppermute | solution.py:445
